TPU v7x, 32 devices: a whole 2x2x4 slice. The times are simulated.
32 devices in a mesh: fsdp: 4 (over z), replica: 2 (over x), ctx: 4 (over y, core).
Axes of the slice: x: 2, y: 2, z: 4, core: 2. Of those that a mesh axis runs over, the one named last changes fastest.
Arguments:
- hidden_in: bfloat16 [8, 1088, 2048], P(('fsdp', 'replica'), 'ctx'), may hold values from -6 to 6
- memory_rows: bfloat16 [8, 50, 2048], P(('fsdp', 'replica')), may hold values from -6 to 6
- seg_len: int32 [8], P(('fsdp', 'replica')), may hold values from 519 to 1038, as said below
- out_grad: bfloat16 [8, 1088, 2048], P(('fsdp', 'replica'), 'ctx'), may hold values from -6 to 6
- first_gain: bfloat16 [2048], P('fsdp'), may hold values from 0.5 to 1.5
- first_shift: bfloat16 [2048], P('fsdp'), may hold values from -1 to 1
- qkv_weight: bfloat16 [2048, 6144], P('fsdp'), may hold values from -0.125 to 0.125
- query_bias: bfloat16 [2048], P('fsdp'), may hold values from -4 to 4
- value_bias: bfloat16 [2048], P('fsdp'), may hold values from -2.5 to 2.5
- out_weight: bfloat16 [2048, 2048], P('fsdp'), may hold values from -2 to 2
- out_bias: bfloat16 [2048], P('fsdp'), may hold values from -1 to 1
- second_gain: bfloat16 [2048], P('fsdp'), may hold values from 0.5 to 1.5
- second_shift: bfloat16 [2048], P('fsdp'), may hold values from -1 to 1
- up_weight: bfloat16 [2048, 8192], P('fsdp'), may hold values from -0.125 to 0.125
- up_bias: bfloat16 [8192], P('fsdp'), may hold values from -1 to 1
- down_weight: bfloat16 [8192, 2048], P('fsdp'), may hold values from -0.0625 to 0.0625
- down_bias: bfloat16 [2048], P('fsdp'), may hold values from -1 to 1
Outputs:
- output: bfloat16 [8, 1088, 2048], P(('fsdp', 'replica'), 'ctx')
- input_grad: float32 [8, 1088, 2048], P(('fsdp', 'replica'), 'ctx')
- memory_grad: float32 [8, 50, 2048], P(('fsdp', 'replica'))
- first_gain_grad: float32 [2048], P('fsdp')
- first_shift_grad: float32 [2048], P('fsdp')
- qkv_weight_grad: float32 [2048, 6144], P('fsdp')
- query_bias_grad: float32 [2048], P('fsdp')
- value_bias_grad: float32 [2048], P('fsdp')
- out_weight_grad: float32 [2048, 2048], P('fsdp')
- out_bias_grad: float32 [2048], P('fsdp')
- second_gain_grad: float32 [2048], P('fsdp')
- second_shift_grad: float32 [2048], P('fsdp')
- up_weight_grad: float32 [2048, 8192], P('fsdp')
- up_bias_grad: float32 [8192], P('fsdp')
- down_weight_grad: float32 [8192, 2048], P('fsdp')
- down_bias_grad: float32 [2048], P('fsdp')
Inputs may be any that keep to these rules, and one draw needn't show every extreme that they name: Positions seg_len to 1037 of a segment are padding that no query uses as a key.
All inputs are finite; a program needn't handle non-finite values.
Results may differ from a plain program's by a relative error of at most 0.015.
Values may be sent and summed in bfloat16 or wider, within the bound.
No kernel may reach another device: no remote copies, remote signals or barrier semaphores. Data moves between devices by JAX's collectives and lax.ppermute only.
A program may use at most 512 MiB of HBM per device.

v0:
```python
import jax
import jax.numpy as jnp
from jax import lax
from jax.sharding import PartitionSpec as P

D = 2048
HEADS = 32
HEAD_DIM = 64
SUMM = 50
SEQ_LEN = 1088
SEG = 1038
epsilon = 1e-05
masked = -1e30


def smooth_unit(values):
    return jax.nn.gelu(values, approximate=False)


def layer_norm(inputs, weight, offset):
    average = jnp.mean(inputs, axis=-1, keepdims=True)
    centred = inputs - average
    spread = jnp.mean(centred * centred, axis=-1, keepdims=True)
    inverse = lax.rsqrt(spread + epsilon)
    normal = centred * inverse
    return (normal * weight + offset, normal, inverse)


def norm_back(upstream, normal, inverse, weight):
    scaled = upstream * weight
    centre_term = jnp.mean(scaled, axis=-1, keepdims=True)
    slope_term = jnp.mean(scaled * normal, axis=-1, keepdims=True)
    return (
        inverse * (scaled - centre_term - normal * slope_term),
        jnp.sum(upstream * normal, axis=0),
        jnp.sum(upstream, axis=0),
    )


def across(left, right):
    return lax.dot_general(
        left, right, (((0,), (0,)), ((), ())), preferred_element_type=jnp.float32
    )


def against(left, right):
    return lax.dot_general(
        left, right, (((1,), (1,)), ((), ())), preferred_element_type=jnp.float32
    )


def head_slice(array, block_index, block_width, head_group):
    piece = lax.dynamic_slice_in_dim(array, block_index * block_width, block_width, 2)
    return piece.reshape(piece.shape[0], piece.shape[1], head_group, block_width // head_group)


def shards(
    hidden_in,
    memory_rows,
    seg_len,
    out_grad,
    first_gain,
    first_shift,
    qkv_weight,
    query_bias,
    value_bias,
    out_weight,
    out_bias,
    second_gain,
    second_shift,
    up_weight,
    up_bias,
    down_weight,
    down_bias,
):
    gathered = (
        lax.all_gather(first_gain, "fsdp", axis=0, tiled=True),
        lax.all_gather(first_shift, "fsdp", axis=0, tiled=True),
        lax.all_gather(qkv_weight, "fsdp", axis=0, tiled=True),
        lax.all_gather(query_bias, "fsdp", axis=0, tiled=True),
        lax.all_gather(value_bias, "fsdp", axis=0, tiled=True),
        lax.all_gather(out_weight, "fsdp", axis=0, tiled=True),
        lax.all_gather(out_bias, "fsdp", axis=0, tiled=True),
        lax.all_gather(second_gain, "fsdp", axis=0, tiled=True),
        lax.all_gather(second_shift, "fsdp", axis=0, tiled=True),
        lax.all_gather(up_weight, "fsdp", axis=0, tiled=True),
        lax.all_gather(up_bias, "fsdp", axis=0, tiled=True),
        lax.all_gather(down_weight, "fsdp", axis=0, tiled=True),
        lax.all_gather(down_bias, "fsdp", axis=0, tiled=True),
    )
    gain_one = gathered[0].astype(jnp.float32)
    shift_one = gathered[1].astype(jnp.float32)
    bias_query = gathered[3].astype(jnp.float32)
    bias_value = gathered[4].astype(jnp.float32)
    bias_out = gathered[6].astype(jnp.float32)
    gain_two = gathered[7].astype(jnp.float32)
    shift_two = gathered[8].astype(jnp.float32)
    bias_up = gathered[10].astype(jnp.float32)
    bias_down = gathered[12].astype(jnp.float32)
    weight_qkv = gathered[2]
    weight_out = gathered[5]
    weight_up = gathered[9]
    weight_down = gathered[11]
    groups = hidden_in.shape[0]
    span_rows = hidden_in.shape[1]
    row_count = groups * span_rows
    mem_count = groups * SUMM
    key_count = SUMM + SEQ_LEN
    head_group = min(8, HEADS)
    group_count = HEADS // head_group
    block_width = head_group * HEAD_DIM
    tokens = hidden_in.reshape(row_count, D).astype(jnp.float32)
    normed, normal_one, inverse_one = layer_norm(tokens, gain_one, shift_one)
    normed_low = normed.astype(jnp.bfloat16)
    memory = memory_rows.reshape(mem_count, D).astype(jnp.float32)
    mem_normed, mem_normal, mem_inverse = layer_norm(memory, gain_one, shift_one)
    mem_low = mem_normed.astype(jnp.bfloat16)
    projected = jnp.dot(normed_low, weight_qkv, preferred_element_type=jnp.float32)
    mem_projected = jnp.dot(mem_low, weight_qkv[:, D:], preferred_element_type=jnp.float32)
    query = (
        ((projected[:, :D] + bias_query) * 0.125).astype(jnp.bfloat16).reshape(groups, span_rows, D)
    )
    keys_local = projected[:, D : 2 * D].astype(jnp.bfloat16).reshape(groups, span_rows, D)
    values_local = (
        (projected[:, 2 * D :] + bias_value).astype(jnp.bfloat16).reshape(groups, span_rows, D)
    )
    mem_keys = mem_projected[:, :D].astype(jnp.bfloat16).reshape(groups, SUMM, D)
    mem_values = (mem_projected[:, D:] + bias_value).astype(jnp.bfloat16).reshape(groups, SUMM, D)
    keys_seq, values_seq = (
        lax.all_gather(keys_local, "ctx", axis=1, tiled=True),
        lax.all_gather(values_local, "ctx", axis=1, tiled=True),
    )
    keys_all = jnp.concatenate([mem_keys, keys_seq], axis=1)
    values_all = jnp.concatenate([mem_values, values_seq], axis=1)
    positions = lax.axis_index("ctx") * span_rows + jnp.arange(span_rows, dtype=jnp.int32)
    key_places = jnp.arange(SEQ_LEN, dtype=jnp.int32)
    causal = key_places[None, :] <= positions[:, None]
    present = (key_places[None, :] < seg_len[:, None]) | (key_places[None, :] >= SEG)
    allowed = jnp.concatenate(
        [jnp.ones((groups, span_rows, SUMM), dtype=bool), causal[None] & present[:, None, :]],
        axis=2,
    )[:, None]

    def attend(block_index):
        query_block = head_slice(query, block_index, block_width, head_group)
        key_block = head_slice(keys_all, block_index, block_width, head_group)
        value_block = head_slice(values_all, block_index, block_width, head_group)
        scores = jnp.einsum(
            "gqhd,gkhd->ghqk", query_block, key_block, preferred_element_type=jnp.float32
        )
        scores = jnp.where(allowed, scores, masked)
        largest = jnp.max(scores, axis=-1, keepdims=True)
        expanded = jnp.exp(scores - largest)
        totals = jnp.sum(expanded, axis=-1, keepdims=True)
        weights_low = (expanded / totals).astype(jnp.bfloat16)
        mixed_rows = jnp.einsum(
            "ghqk,gkhd->gqhd", weights_low, value_block, preferred_element_type=jnp.float32
        )
        return (mixed_rows.reshape(groups, span_rows, block_width), largest + jnp.log(totals))

    mixed_blocks, log_totals = lax.map(attend, jnp.arange(group_count))
    attended = jnp.moveaxis(mixed_blocks, 0, 2).reshape(row_count, D).astype(jnp.bfloat16)
    branch = jnp.dot(attended, weight_out, preferred_element_type=jnp.float32) + bias_out
    middle = tokens + branch
    normed_two, normal_two, inverse_two = layer_norm(middle, gain_two, shift_two)
    normed_two_low = normed_two.astype(jnp.bfloat16)
    upper = jnp.dot(normed_two_low, weight_up, preferred_element_type=jnp.float32) + bias_up
    active_float, smooth_pull = jax.vjp(smooth_unit, upper)
    active = active_float.astype(jnp.bfloat16)
    output = (
        (middle + (jnp.dot(active, weight_down, preferred_element_type=jnp.float32) + bias_down))
        .astype(jnp.bfloat16)
        .reshape(groups, span_rows, D)
    )
    again = (
        lax.all_gather(qkv_weight, "fsdp", axis=0, tiled=True),
        lax.all_gather(out_weight, "fsdp", axis=0, tiled=True),
        lax.all_gather(up_weight, "fsdp", axis=0, tiled=True),
        lax.all_gather(down_weight, "fsdp", axis=0, tiled=True),
    )
    back_qkv = again[0]
    back_out = again[1]
    back_up = again[2]
    back_down = again[3]
    cotangent = out_grad.reshape(row_count, D)
    cot_float = cotangent.astype(jnp.float32)
    down_part = lax.psum_scatter(
        across(active, cotangent).astype(jnp.bfloat16), "fsdp", scatter_dimension=0, tiled=True
    ).astype(jnp.float32)
    hidden_grad = against(cotangent, back_down)
    upper_grad = smooth_pull(hidden_grad)[0].astype(jnp.bfloat16)
    up_part = lax.psum_scatter(
        across(normed_two_low, upper_grad).astype(jnp.bfloat16),
        "fsdp",
        scatter_dimension=0,
        tiled=True,
    ).astype(jnp.float32)
    normed_two_grad = against(upper_grad, back_up)
    middle_norm_grad, gain_two_grad, shift_two_grad = norm_back(
        normed_two_grad, normal_two, inverse_two, gain_two
    )
    middle_grad = cot_float + middle_norm_grad
    branch_grad = middle_grad.astype(jnp.bfloat16)
    out_weight_grad = across(attended, branch_grad)
    mixed_grad = against(branch_grad, back_out).astype(jnp.bfloat16).reshape(groups, span_rows, D)

    def attend_back(block_index):
        query_block = head_slice(query, block_index, block_width, head_group)
        key_block = head_slice(keys_all, block_index, block_width, head_group)
        value_block = head_slice(values_all, block_index, block_width, head_group)
        grad_block = head_slice(mixed_grad, block_index, block_width, head_group)
        scores = jnp.einsum(
            "gqhd,gkhd->ghqk", query_block, key_block, preferred_element_type=jnp.float32
        )
        scores = jnp.where(allowed, scores, masked)
        weights = jnp.exp(scores - log_totals[block_index])
        value_grad = jnp.einsum(
            "ghqk,gqhd->gkhd",
            weights.astype(jnp.bfloat16),
            grad_block,
            preferred_element_type=jnp.float32,
        )
        weight_grad = jnp.einsum(
            "gqhd,gkhd->ghqk", grad_block, value_block, preferred_element_type=jnp.float32
        )
        centre = jnp.sum(weights * weight_grad, axis=-1, keepdims=True)
        score_grad = (weights * (weight_grad - centre)).astype(jnp.bfloat16)
        query_grad = jnp.einsum(
            "ghqk,gkhd->gqhd", score_grad, key_block, preferred_element_type=jnp.float32
        )
        key_grad = jnp.einsum(
            "ghqk,gqhd->gkhd", score_grad, query_block, preferred_element_type=jnp.float32
        )
        return (
            query_grad.reshape(groups, span_rows, block_width),
            key_grad.reshape(groups, key_count, block_width),
            value_grad.reshape(groups, key_count, block_width),
        )

    query_blocks, key_blocks, value_blocks = lax.map(attend_back, jnp.arange(group_count))
    query_grad_all = jnp.moveaxis(query_blocks, 0, 2).reshape(groups, span_rows, D)
    key_grad_all = jnp.moveaxis(key_blocks, 0, 2).reshape(groups, key_count, D)
    value_grad_all = jnp.moveaxis(value_blocks, 0, 2).reshape(groups, key_count, D)
    key_sums, value_sums = (
        lax.psum_scatter(key_grad_all[:, SUMM:], "ctx", scatter_dimension=1, tiled=True),
        lax.psum_scatter(value_grad_all[:, SUMM:], "ctx", scatter_dimension=1, tiled=True),
    )
    mem_key_sums, mem_value_sums = lax.psum(
        (key_grad_all[:, :SUMM], value_grad_all[:, :SUMM]), "ctx"
    )
    qkv_grad = jnp.concatenate(
        [
            query_grad_all.astype(jnp.bfloat16) * 0.125,
            key_sums.astype(jnp.bfloat16),
            value_sums.astype(jnp.bfloat16),
        ],
        axis=2,
    ).reshape(row_count, 3 * D)
    mem_kv_grad = jnp.concatenate(
        [mem_key_sums.astype(jnp.bfloat16), mem_value_sums.astype(jnp.bfloat16)], axis=2
    ).reshape(mem_count, 2 * D)
    owner_flag = lax.axis_index("ctx") == 0
    first_owner = owner_flag.astype(jnp.float32)
    owned_mem_grad = jnp.where(owner_flag, mem_kv_grad, jnp.zeros_like(mem_kv_grad))
    mem_rows_grad = jnp.concatenate(
        [jnp.zeros((mem_count, D), jnp.bfloat16), owned_mem_grad], axis=1
    )
    qkv_weight_grad = across(
        jnp.concatenate([normed_low, mem_low], axis=0),
        jnp.concatenate([qkv_grad, mem_rows_grad], axis=0),
    )
    query_bias_grad = jnp.sum(qkv_grad[:, :D].astype(jnp.float32), axis=0)
    value_bias_grad = jnp.sum(qkv_grad[:, 2 * D :].astype(jnp.float32), axis=0) + jnp.sum(
        owned_mem_grad[:, D:].astype(jnp.float32), axis=0
    )
    out_bias_grad = jnp.sum(branch_grad.astype(jnp.float32), axis=0)
    up_bias_grad = jnp.sum(upper_grad.astype(jnp.float32), axis=0)
    down_bias_grad = jnp.sum(cot_float, axis=0)
    normed_grad = against(qkv_grad, back_qkv)
    token_norm_grad, gain_one_tok, shift_one_tok = norm_back(
        normed_grad, normal_one, inverse_one, gain_one
    )
    mem_normed_grad = against(mem_kv_grad, back_qkv[:, D:])
    memory_norm_grad, gain_one_mem, shift_one_mem = norm_back(
        mem_normed_grad, mem_normal, mem_inverse, gain_one
    )
    gain_one_grad = gain_one_tok + first_owner * gain_one_mem
    shift_one_grad = shift_one_tok + first_owner * shift_one_mem
    input_grad = (middle_grad + token_norm_grad).reshape(groups, span_rows, D)
    memory_grad = memory_norm_grad.reshape(groups, SUMM, D)
    shares = (
        lax.psum_scatter(
            gain_one_grad.astype(jnp.bfloat16), "fsdp", scatter_dimension=0, tiled=True
        ).astype(jnp.float32),
        lax.psum_scatter(
            shift_one_grad.astype(jnp.bfloat16), "fsdp", scatter_dimension=0, tiled=True
        ).astype(jnp.float32),
        lax.psum_scatter(
            qkv_weight_grad.astype(jnp.bfloat16), "fsdp", scatter_dimension=0, tiled=True
        ).astype(jnp.float32),
        lax.psum_scatter(
            query_bias_grad.astype(jnp.bfloat16), "fsdp", scatter_dimension=0, tiled=True
        ).astype(jnp.float32),
        lax.psum_scatter(
            value_bias_grad.astype(jnp.bfloat16), "fsdp", scatter_dimension=0, tiled=True
        ).astype(jnp.float32),
        lax.psum_scatter(
            out_weight_grad.astype(jnp.bfloat16), "fsdp", scatter_dimension=0, tiled=True
        ).astype(jnp.float32),
        lax.psum_scatter(
            out_bias_grad.astype(jnp.bfloat16), "fsdp", scatter_dimension=0, tiled=True
        ).astype(jnp.float32),
        lax.psum_scatter(
            gain_two_grad.astype(jnp.bfloat16), "fsdp", scatter_dimension=0, tiled=True
        ).astype(jnp.float32),
        lax.psum_scatter(
            shift_two_grad.astype(jnp.bfloat16), "fsdp", scatter_dimension=0, tiled=True
        ).astype(jnp.float32),
        lax.psum_scatter(
            up_bias_grad.astype(jnp.bfloat16), "fsdp", scatter_dimension=0, tiled=True
        ).astype(jnp.float32),
        lax.psum_scatter(
            down_bias_grad.astype(jnp.bfloat16), "fsdp", scatter_dimension=0, tiled=True
        ).astype(jnp.float32),
    )
    summed = lax.psum(
        (
            shares[0],
            shares[1],
            shares[2],
            shares[3],
            shares[4],
            shares[5],
            shares[6],
            shares[7],
            shares[8],
            shares[9],
            shares[10],
            up_part,
            down_part,
        ),
        ("replica", "ctx"),
    )
    return (
        output,
        input_grad,
        memory_grad,
        summed[0],
        summed[1],
        summed[2],
        summed[3],
        summed[4],
        summed[5],
        summed[6],
        summed[7],
        summed[8],
        summed[11],
        summed[9],
        summed[12],
        summed[10],
    )


def solution(mesh):
    return jax.shard_map(
        shards,
        mesh=mesh,
        in_specs=(
            P(("fsdp", "replica"), "ctx", None),
            P(("fsdp", "replica"), None, None),
            P(("fsdp", "replica")),
            P(("fsdp", "replica"), "ctx", None),
            P("fsdp"),
            P("fsdp"),
            P("fsdp", None),
            P("fsdp"),
            P("fsdp"),
            P("fsdp", None),
            P("fsdp"),
            P("fsdp"),
            P("fsdp"),
            P("fsdp", None),
            P("fsdp"),
            P("fsdp", None),
            P("fsdp"),
        ),
        out_specs=(
            P(("fsdp", "replica"), "ctx", None),
            P(("fsdp", "replica"), "ctx", None),
            P(("fsdp", "replica"), None, None),
            P("fsdp"),
            P("fsdp"),
            P("fsdp", None),
            P("fsdp"),
            P("fsdp"),
            P("fsdp", None),
            P("fsdp"),
            P("fsdp"),
            P("fsdp"),
            P("fsdp", None),
            P("fsdp"),
            P("fsdp", None),
            P("fsdp"),
        ),
        check_vma=False,
    )
```

profile of v0, /device:TPU:1, one launch (start us, length us, event | category | flops | bytes accessed | tf_op | source)
XLA Modules:
  0.0 7154.1 jit_solution(2888771679025506342)
XLA Ops:
  8.7 10.3 all-gather.3
  19.7 9.3 all-gather.2
  29.7 36.0 all-gather.5
  66.3 33.2 all-gather.4
  100.8 336.6 %all-gather.17.cloned.1.call-done = bf16[2048,6144]{1,0:T(8,128)(2,1)} async-done(((bf16[512,6144]{1,0:T(8,128)(2,1)}), bf16[2048,6144]{1,0:T(8,128)(2,1)}) %all-gather.17.cloned.1.call-update) | async-done | bytes 25165840 | tf_op jit(solution)/shard_map/all_gather | solution.py:79
  437.4 11.9 fusion.87
  458.9 9.7 all-gather.6
  469.3 10.2 all_gather.61
  479.6 9.7 all-gather.8
  489.3 9.3 all-gather.7
  503.1 7.4 fusion.7
  516.6 6.7 copy.54
  532.8 6.9 copy.56
  540.9 48.0 while.26
  589.0 88.8 %all-gather.19.cloned.1.call-done = bf16[2048,2048]{1,0:T(8,128)(2,1)} async-done(((bf16[512,2048]{1,0:T(8,128)(2,1)}), bf16[2048,2048]{1,0:T(8,128)(2,1)}) %all-gather.19.cloned.1.call-update) | async-done | bytes 8388624 | tf_op jit(solution)/shard_map/all_gather | solution.py:82
  677.7 6.6 fusion.82
  686.1 552.7 %all-gather.21.cloned.1.call-done = bf16[2048,8192]{1,0:T(8,128)(2,1)} async-done(((bf16[512,8192]{1,0:T(8,128)(2,1)}), bf16[2048,8192]{1,0:T(8,128)(2,1)}) %all-gather.21.cloned.1.call-update) | async-done | bytes 33554448 | tf_op jit(solution)/shard_map/all_gather | solution.py:86
  1238.8 34.7 multiply_convert_fusion.1
  1273.5 526.4 %all-gather.23.cloned.1.call-done = bf16[8192,2048]{1,0:T(8,128)(2,1)} async-done(((bf16[2048,2048]{1,0:T(8,128)(2,1)}), bf16[8192,2048]{1,0:T(8,128)(2,1)}) %all-gather.23.cloned.1.call-update) | async-done | bytes 33554448 | tf_op jit(solution)/shard_map/all_gather | solution.py:88
  1799.8 36.5 fusion.83
  1836.4 17.0 multiply_reduce_fusion.1
  1854.9 6.8 convolution_convert_fusion.3
  1862.0 6.9 fusion.32
  1870.2 188.6 %while.27 = (s32[]{:T(128)}, bf16[4,1,272,512]{2,3,1,0:T(8,128)(2,1)}, f32[4,1,1138,512]{2,3,1,0:T(8,128)}, f32[4,1,1138,512]{2,3,1,0:T(8,128)}, s32[4]{0:T(128)...) while((s32[]{:T(128)}, ...), condition=%wide.region_14.15_spmd, body=%wide.region_12.14_spmd.sunk | while | flops 1604632448 | bytes 115616344 | solution.py:240
  1884.6 8.4 multiply_reduce_fusion.8
  1893.0 10.1 multiply_convert_fusion.3
  1931.8 8.3 multiply_reduce_fusion.8
  1940.1 10.1 multiply_convert_fusion.3
  1978.8 8.4 multiply_reduce_fusion.8
  1987.2 10.1 multiply_convert_fusion.3
  2026.1 8.3 multiply_reduce_fusion.8
  2034.4 10.0 multiply_convert_fusion.3
  2060.4 10.1 slice.62
  2077.8 21.4 copy.74
  2099.3 21.4 copy.73
  2120.7 2492.1 %all-reduce.20 = (bf16[1,50,2048]{2,0,1:T(2,128)(2,1)S(1)}, bf16[1,50,2048]{2,0,1:T(2,128)(2,1)S(1)}, bf16[1,1088,2048]{2,0,1:T(2,128)(2,1)}, bf16[1,1088,2048]{2,0,1:T(2,128)(2,1)}) all-reduce(f32[1,50,2048]{2,0,1:T(1,128)S(1)} %copy.76, f32[1,50,2048]{2,0,1:T(1,128)S(1)} %copy.75, ...), channel_id=1, replica_groups=mesh['fsdp'=4,'replica'=2,'ctx'=4] {'ctx'}, use_global_device_ids=true, to_apply=%region_20.21 | all-reduce | flops 4661248 | bytes 27967488 | tf_op jit(solution)/shard_map/psum | solution.py:248
  4629.4 17.2 convolution_convert_fusion.2
  4648.3 24.3 convolution_convert_fusion.1
  4673.8 24.3 convolution_convert_fusion
  4698.8 11.8 all-gather.9
  4712.8 12.2 fusion.69
  4731.5 14.9 fusion.40
  4746.5 19.0 all-reduce.17
  4770.6 17.5 fusion.31
  4788.1 272.3 %reduce-scatter.9.cloned.1.call-done = bf16[512,6144]{1,0:T(8,128)(2,1)} async-done(((bf16[2048,6144]{1,0:T(8,128)(2,1)}), bf16[512,6144]{1,0:T(8,128)(2,1)}) %reduce-scatter.9.cloned.1.call-update) | async-done | bytes 6291472 | tf_op jit(solution)/shard_map/reduce_scatter | solution.py:298
  5060.4 556.3 %reduce-scatter.13.cloned.1.call-done = bf16[512,8192]{1,0:T(8,128)(2,1)} async-done(((bf16[2048,8192]{1,0:T(8,128)(2,1)}), bf16[512,8192]{1,0:T(8,128)(2,1)}) %reduce-scatter.13.cloned.1.call-update) | async-done | bytes 8388624
  5616.7 555.0 %reduce-scatter.15.cloned.1.call-done = bf16[2048,2048]{1,0:T(8,128)(2,1)} async-done(((bf16[8192,2048]{1,0:T(8,128)(2,1)}), bf16[2048,2048]{1,0:T(8,128)(2,1)}) %reduce-scatter.15.cloned.1.call-update) | async-done | bytes 8388624
  6171.8 975.3 %all-reduce.21 = (f32[512]{0:T(512)}, f32[512]{0:T(512)}, f32[512,6144]{1,0:T(8,128)}, f32[512]{0:T(512)}, f32[512]{0:T(512)}, /*index=5*/f32[512,2048]{1,0:T(8,...) all-reduce(f32[512]{0:T(512)S(1)} %dynamic-slice_convert_fusion.8, ...), channel_id=1, replica_groups=mesh['fsdp'=4,'replica'=2,'ctx'=4] {'replica','ctx'}, use_global_device_ids=true, to_apply=%region_26.27 | all-reduce | flops 12589056 | bytes 75546624 | tf_op jit(solution)/shard_map/psum | solution.py:326
  (332 shorter events, 229.7 us)
Async XLA Ops:
  7.2 92.4 %copy-start.2 = (bf16[1,272,2048]{2,1,0:T(8,128)(2,1)S(1)}, bf16[1,272,2048]{2,1,0:T(8,128)(2,1)}, u32[]{:S(2)}) copy-start(bf16[1,272,2048]{2,1,0:T(8,128)(2,1)} %param.21) | copy-start | bytes 3342340
  7.2 430.2 %all-gather.17.cloned.1.call-start = ((), (), s32[]{:S(2)}) async-start(), calls=%async_computation.4 | async-start | bytes 31457280 | tf_op jit(solution)/shard_map/all_gather | solution.py:79
  7.9 502.7 %all-gather.25.cloned.1.call-start = ((), (), s32[]{:S(2)}) async-start(), calls=%async_computation.10 | async-start | bytes 5570560 | tf_op jit(solution)/shard_map/all_gather | solution.py:131
  29.0 472.0 %copy-start.25 = (f32[4,1,512]{2,1,0:T(1,128)}, f32[4,1,512]{2,1,0:T(1,128)S(1)}, u32[]{:S(2)}) copy-start(f32[4,1,512]{2,1,0:T(1,128)S(1)} %convert_element_type.263) | copy-start | bytes 24580
  99.8 349.5 %copy-start.29 = (f32[272]{0:T(512)}, f32[272]{0:T(512)S(1)}, u32[]{:S(2)}) copy-start(f32[272]{0:T(512)S(1)} %broadcast_multiply_fusion.5) | copy-start | bytes 3268
  100.3 349.1 %copy-start.33 = (f32[272]{0:T(512)}, f32[272]{0:T(512)S(1)}, u32[]{:S(2)}) copy-start(f32[272]{0:T(512)S(1)} %add_rsqrt_fusion.1) | copy-start | bytes 3268
  100.8 348.6 %copy-start.18 = (bf16[272,2048]{1,0:T(8,128)(2,1)}, bf16[272,2048]{1,0:T(8,128)(2,1)S(1)}, u32[]{:S(2)}) copy-start(bf16[272,2048]{1,0:T(8,128)(2,1)S(1)} %fusion.34) | copy-start | bytes 3342340
  454.2 72.7 %all-gather.27.cloned.1.call-start = ((), (), s32[]{:S(2)}) async-start(), calls=%async_computation.11 | async-start | bytes 5570560 | tf_op jit(solution)/shard_map/all_gather | solution.py:130
  457.0 220.7 %all-gather.19.cloned.1.call-start = ((), (), s32[]{:S(2)}) async-start(), calls=%async_computation.5 | async-start | bytes 10485760 | tf_op jit(solution)/shard_map/all_gather | solution.py:82
  457.6 11.7 copy-start.43
  457.6 21.9 copy-start.49
  457.6 31.6 copy-start.50
  457.6 41.0 copy-start.53
  457.7 42.2 copy-start.17
  457.7 781.1 %all-gather.21.cloned.1.call-start = ((), (), s32[]{:S(2)}) async-start(), calls=%async_computation.6 | async-start | bytes 41943040 | tf_op jit(solution)/shard_map/all_gather | solution.py:86
  458.3 1341.6 %all-gather.23.cloned.1.call-start = ((), (), s32[]{:S(2)}) async-start(), calls=%async_computation.7 | async-start | bytes 41943040 | tf_op jit(solution)/shard_map/all_gather | solution.py:88
  458.8 4329.3 %reduce-scatter.11.cloned.1.call-start = ((), (), s32[]{:S(2)}) async-start(), calls=%async_computation.9 | async-start | bytes 10485760 | tf_op jit(solution)/shard_map/reduce_scatter | solution.py:307
  489.3 749.5 %copy-start.39 = (f32[4,1,512]{2,1,0:T(1,128)}, f32[4,1,512]{2,1,0:T(1,128)S(1)}, u32[]{:S(2)}) copy-start(f32[4,1,512]{2,1,0:T(1,128)S(1)} %convert_element_type.269) | copy-start | bytes 24580
  498.6 1354.8 %copy-start.27 = (f32[4,1,512]{2,1,0:T(1,128)}, f32[4,1,512]{2,1,0:T(1,128)S(1)}, u32[]{:S(2)}) copy-start(f32[4,1,512]{2,1,0:T(1,128)S(1)} %convert_element_type.268) | copy-start | bytes 24580
  500.0 10.5 copy-start.41
  500.3 10.2 copy-start.46
  589.0 95.4 %copy-start = (pred[1,1,272,1138]{3,2,1,0:T(8,128)(4,1)}, pred[1,1,272,1138]{3,2,1,0:T(8,128)(4,1)S(1)}, u32[]{:S(2)}) copy-start(pred[1,1,272,1138]{3,2,1,0:T(8,128)(4,1)S(1)} %get-tuple-element.553) | copy-start | bytes 928612
  589.0 95.4 %copy-start.7 = (bf16[1,272,2048]{1,2,0:T(8,128)(2,1)}, bf16[1,272,2048]{1,2,0:T(8,128)(2,1)S(1)}, u32[]{:S(2)}) copy-start(bf16[1,272,2048]{1,2,0:T(8,128)(2,1)S(1)} %get-tuple-element.562) | copy-start | bytes 3342340
  684.4 1169.1 %copy-start.31 = (f32[272]{0:T(512)}, f32[272]{0:T(512)S(1)}, u32[]{:S(2)}) copy-start(f32[272]{0:T(512)S(1)} %broadcast_multiply_fusion.4) | copy-start | bytes 3268
  686.1 1167.3 %copy-start.37 = (f32[272]{0:T(512)}, f32[272]{0:T(512)S(1)}, u32[]{:S(2)}) copy-start(f32[272]{0:T(512)S(1)} %add_rsqrt_fusion) | copy-start | bytes 3268
  1238.8 561.0 %copy-start.13 = (bf16[1,272,2048]{2,1,0:T(8,128)(2,1)S(1)}, bf16[1,272,2048]{2,1,0:T(8,128)(2,1)}, u32[]{:S(2)}) copy-start(bf16[1,272,2048]{2,1,0:T(8,128)(2,1)} %param.24) | copy-start | bytes 3342340
  1799.8 36.5 copy-start.5
  1836.4 17.1 copy-start.14
  1854.9 7.1 copy-start.9
  1861.8 8.4 copy-start.1
  1861.8 3198.6 %reduce-scatter.9.cloned.1.call-start = ((), (), s32[]{:S(2)}) async-start(), calls=%async_computation.8 | async-start | bytes 31457280 | tf_op jit(solution)/shard_map/reduce_scatter | solution.py:298
  2058.9 11.6 slice-start.2
  2060.3 10.1 slice-start.3
  2060.3 10.1 slice-start.4
  4617.4 8.2 copy-start.16
  4646.7 970.0 %reduce-scatter.13.cloned.1.call-start = ((), (), s32[]{:S(2)}) async-start(), calls=%async_computation.12 | async-start | bytes 41943040
  4672.6 1499.1 %reduce-scatter.15.cloned.1.call-start = ((), (), s32[]{:S(2)}) async-start(), calls=%async_computation.13 | async-start | bytes 41943040
  4698.1 12.7 copy-start.52
  4698.1 14.6 copy-start.26
  4698.1 14.6 copy-start.42
  4698.2 14.6 copy-start.47
  4712.8 18.7 copy-start.3
  4712.8 18.7 copy-start.30
  4712.8 18.7 copy-start.34
  4731.5 15.0 copy-start.35
  4731.5 15.0 copy-start.36
  4731.5 15.0 copy-start.44
  4731.5 15.0 copy-start.45
  (27 other events, 90.5 us)
Sparse Core Ops, SparseCore 0:
  9.6 427.7 all-gather.16
  454.3 34.3 all-gather.24
  490.8 35.9 all-gather.26
  528.2 149.4 all-gather.18
  679.1 559.6 all-gather.20
  1240.2 559.5 all-gather.22
  1861.9 142.2 reduce-scatter.10
  4646.8 413.5 reduce-scatter.8
  5062.9 553.7 reduce-scatter.12
  5619.0 552.7 reduce-scatter.14
where the time goes:
time: 7170 us; the launch traced here: 7150 us
  blocking collectives  3630 us (51%)
  waiting for transfers between devices  2890 us (40%)
  matrix products  356 us (5%)
  local copies, waits for them, and re-layouts  161 us (2%)
  other arithmetic  84.4 us (1%)
    psum x1, blocking collectives, shards(): lax.psum((key_grad_all[:, :SUMM], value_grad_all[:, :SUMM]), 'ctx')  2490 us
    unnamed x12, waiting for transfers between devices  1110 us
    psum x1, blocking collectives, shards(): lax.psum((shares[0], shares[1], shares[2], shares[3], shares[4], shares[5...  975 us
    all_gather x1, waiting for transfers between devices, shards(): lax.all_gather(up_weight, 'fsdp', axis=0, tiled=True)  553 us
    all_gather x1, waiting for transfers between devices, shards(): lax.all_gather(down_weight, 'fsdp', axis=0, tiled=True)  526 us
    all_gather x1, waiting for transfers between devices, shards(): lax.all_gather(qkv_weight, 'fsdp', axis=0, tiled=True)  337 us
    reduce_scatter x1, waiting for transfers between devices, shards(): lax.psum_scatter(qkv_weight_grad.astype(jnp.bfloat16), 'fsdp', scatter_di...  272 us
  transfers between devices with their start and end apart: 10, of which 8 were waited for; matrix products, arithmetic and copies ran while one was open for 7% of the time, Pallas kernels for 0%

commit v1 on v0

--- a/solution.py
+++ b/solution.py
@@ -11,6 +11,19 @@
 SEG = 1038
 epsilon = 1e-05
 masked = -1e30
+
+
+def gather_around(x, axis, dim):
+    ways = lax.axis_size(axis)
+    up = [(d, (d + 1) % ways) for d in range(ways)]
+    down = [(d, (d - 1) % ways) for d in range(ways)]
+    earlier, later = ([x], [x])
+    for _ in range(ways // 2):
+        earlier.append(lax.ppermute(earlier[-1], axis, up))
+    for _ in range((ways - 1) // 2):
+        later.append(lax.ppermute(later[-1], axis, down))
+    line = jnp.concatenate([*earlier[::-1], *later[1:]], axis=dim)
+    return jnp.roll(line, (lax.axis_index(axis) - ways // 2) * x.shape[dim], axis=dim)
 
 
 def smooth_unit(values):
@@ -85,7 +98,7 @@
         lax.all_gather(second_shift, "fsdp", axis=0, tiled=True),
         lax.all_gather(up_weight, "fsdp", axis=0, tiled=True),
         lax.all_gather(up_bias, "fsdp", axis=0, tiled=True),
-        lax.all_gather(down_weight, "fsdp", axis=0, tiled=True),
+        gather_around(down_weight, "fsdp", 0),
         lax.all_gather(down_bias, "fsdp", axis=0, tiled=True),
     )
     gain_one = gathered[0].astype(jnp.float32)

time: 7170 us -> 7710 us (1.075)
  blocking collectives: 3630 us -> 4110 us
  local copies, waits for them, and re-layouts: 161 us -> 241 us
    all_gather x1, blocking collectives: 11.8 us -> 495 us  [shards(): lax.all_gather(down_bias, 'fsdp', axis=0, tiled=True)]
    ppermute x0 -> x3, waiting for transfers between devices: none -> 364 us  [the longest x2 364 us: gather_around(): earlier.append(lax.ppermute(earlier[-1], axis, up))]
    reduce_scatter x1, waiting for transfers between devices: 272 us -> 0.01 us  [shards(): lax.psum_scatter(qkv_weight_grad.astype(jnp.bfloat16), 'fsdp', scatter_di...]
    unnamed x12, waiting for transfers between devices: 1110 us -> 972 us
  transfers between devices with their start and end apart: 10 -> 13, of which waited for: 8 -> 8; matrix products, arithmetic and copies ran while one was open for 7% -> 7% of each run, Pallas kernels for 0% -> 0%
where the time goes in v1:
time: 7710 us; the launch traced here: 7690 us
  blocking collectives  4110 us (53%)
  waiting for transfers between devices  2840 us (37%)
  matrix products  341 us (4%)
  local copies, waits for them, and re-layouts  241 us (3%)
  other arithmetic  86.8 us (1%)
    psum x1, blocking collectives, shards(): lax.psum((key_grad_all[:, :SUMM], value_grad_all[:, :SUMM]), 'ctx')  2490 us
    psum x1, blocking collectives, shards(): lax.psum((shares[0], shares[1], shares[2], shares[3], shares[4], shares[5...  975 us
    unnamed x12, waiting for transfers between devices  972 us
    all_gather x1, waiting for transfers between devices, shards(): lax.all_gather(up_weight, 'fsdp', axis=0, tiled=True)  553 us
    all_gather x1, waiting for transfers between devices, shards(): lax.all_gather(down_weight, 'fsdp', axis=0, tiled=True)  526 us
    all_gather x1, blocking collectives, shards(): lax.all_gather(down_bias, 'fsdp', axis=0, tiled=True)  495 us
    ppermute x2, waiting for transfers between devices, gather_around(): earlier.append(lax.ppermute(earlier[-1], axis, up))  364 us
    all_gather x1, waiting for transfers between devices, shards(): lax.all_gather(qkv_weight, 'fsdp', axis=0, tiled=True)  334 us
  transfers between devices with their start and end apart: 13, of which 8 were waited for; matrix products, arithmetic and copies ran while one was open for 7% of the time, Pallas kernels for 0%

profile of v1, /device:TPU:1, one launch (start us, length us, event | category | flops | bytes accessed | tf_op | source)
XLA Modules:
  0.0 7693.5 jit_solution(2250634478453589861)
XLA Ops:
  8.7 10.3 all-gather.2
  19.7 9.3 all-gather.3
  29.7 36.0 all-gather.4
  66.3 33.2 all-gather.5
  103.3 334.1 %all-gather.17.cloned.1.call-done = bf16[2048,6144]{1,0:T(8,128)(2,1)} async-done(((bf16[512,6144]{1,0:T(8,128)(2,1)}), bf16[2048,6144]{1,0:T(8,128)(2,1)}) %all-gather.17.cloned.1.call-update) | async-done | bytes 25165840 | tf_op jit(solution)/shard_map/all_gather | solution.py:92
  437.4 11.9 fusion.99
  459.6 9.7 all-gather.6
  469.3 9.7 all-gather.7
  479.0 9.7 all-gather.8
  488.7 10.2 all_gather.60
  540.9 48.0 while.26
  589.0 88.7 %all-gather.19.cloned.1.call-done = bf16[2048,2048]{1,0:T(8,128)(2,1)} async-done(((bf16[512,2048]{1,0:T(8,128)(2,1)}), bf16[2048,2048]{1,0:T(8,128)(2,1)}) %all-gather.19.cloned.1.call-update) | async-done | bytes 8388624 | tf_op jit(solution)/shard_map/all_gather | solution.py:95
  686.1 552.7 %all-gather.21.cloned.1.call-done = bf16[2048,8192]{1,0:T(8,128)(2,1)} async-done(((bf16[512,8192]{1,0:T(8,128)(2,1)}), bf16[2048,8192]{1,0:T(8,128)(2,1)}) %all-gather.21.cloned.1.call-update) | async-done | bytes 33554448 | tf_op jit(solution)/shard_map/all_gather | solution.py:99
  1238.8 34.7 multiply_convert_fusion.1
  1273.4 526.4 %all-gather.23.cloned.1.call-done = bf16[8192,2048]{1,0:T(8,128)(2,1)} async-done(((bf16[2048,2048]{1,0:T(8,128)(2,1)}), bf16[8192,2048]{1,0:T(8,128)(2,1)}) %all-gather.23.cloned.1.call-update) | async-done | bytes 33554448 | tf_op jit(solution)/shard_map/all_gather | solution.py:192
  1799.8 35.5 fusion.95
  1835.3 17.3 multiply_reduce_fusion.1
  1854.2 8.9 convolution_convert_fusion.3
  1871.6 184.3 %while.27 = (s32[]{:T(128)}, bf16[4,1,272,512]{2,3,1,0:T(8,128)(2,1)}, f32[4,1,1138,512]{2,3,1,0:T(8,128)}, f32[4,1,1138,512]{2,3,1,0:T(8,128)}, s32[4]{0:T(128)...) while((s32[]{:T(128)}, ...), condition=%wide.region_14.15_spmd, body=%wide.region_12.14_spmd.sunk | while | flops 1604632448 | bytes 155238000 | solution.py:253
  1885.9 8.4 multiply_reduce_fusion.8
  1894.3 10.1 multiply_convert_fusion.3
  1932.1 8.4 multiply_reduce_fusion.8
  1940.5 10.1 multiply_convert_fusion.3
  1978.2 8.3 multiply_reduce_fusion.8
  1986.5 10.1 multiply_convert_fusion.3
  2024.2 8.3 multiply_reduce_fusion.8
  2032.5 10.0 multiply_convert_fusion.3
  2055.9 10.1 slice.61
  2073.6 21.4 copy.73
  2095.0 21.4 copy.74
  2117.5 2492.3 %all-reduce.20 = (bf16[1,50,2048]{2,0,1:T(2,128)(2,1)S(1)}, bf16[1,50,2048]{2,0,1:T(2,128)(2,1)S(1)}, bf16[1,1088,2048]{2,0,1:T(2,128)(2,1)}, bf16[1,1088,2048]{2,0,1:T(2,128)(2,1)}) all-reduce(f32[1,50,2048]{2,0,1:T(1,128)S(1)} %copy.76, f32[1,50,2048]{2,0,1:T(1,128)S(1)} %copy.75, ...), channel_id=1, replica_groups=mesh['fsdp'=4,'replica'=2,'ctx'=4] {'ctx'}, use_global_device_ids=true, to_apply=%region_20.21 | all-reduce | flops 4661248 | bytes 27967488 | tf_op jit(solution)/shard_map/psum | solution.py:261
  4626.9 18.3 convolution_convert_fusion.2
  4646.9 24.4 convolution_convert_fusion.1
  4672.5 23.9 convolution_convert_fusion
  4696.5 363.9 %collective-permute-done = bf16[2048,2048]{1,0:T(8,128)(2,1)} collective-permute-done((bf16[2048,2048]{1,0:T(8,128)(2,1)}, bf16[2048,2048]{1,0:T(8,128)(2,1)}, u32[]{:S(2)}, u32[]{:S(2)}) %collective-permute-start) | collective-permute-done | bytes 8388640 | tf_op jit(solution)/shard_map/ppermute | solution.py:22
  5060.3 42.7 collective-permute-start.1
  5106.6 494.9 %all-gather.9 = bf16[4,1,512]{2,1,0:T(2,128)(2,1)S(1)} all-gather(bf16[1,1,512]{2,1,0:T(2,128)(2,1)S(1)} %reshape.399), channel_id=1, replica_groups=mesh['fsdp'=4,'replica'=2,'ctx'=4] {'fsdp'}, dimensions={0}, use_global_device_ids=true | all-gather | bytes 5120 | tf_op jit(solution)/shard_map/all_gather | solution.py:102
  5601.5 8.6 constant_dynamic-update-slice_fusion.11
  5626.6 8.4 constant_dynamic-update-slice_fusion.8
  5635.0 8.3 constant_dynamic-update-slice_fusion.7
  5659.9 8.5 constant_dynamic-update-slice_fusion.4
  5668.4 12.4 fusion.80
  5687.6 14.8 fusion.51
  5702.5 16.6 all-reduce.17
  5724.2 17.7 fusion.40
  5741.9 414.2 %reduce-scatter.13.cloned.1.call-done = bf16[512,8192]{1,0:T(8,128)(2,1)} async-done(((bf16[2048,8192]{1,0:T(8,128)(2,1)}), bf16[512,8192]{1,0:T(8,128)(2,1)}) %reduce-scatter.13.cloned.1.call-update) | async-done | bytes 8388624
  6156.0 555.0 %reduce-scatter.15.cloned.1.call-done = bf16[2048,2048]{1,0:T(8,128)(2,1)} async-done(((bf16[8192,2048]{1,0:T(8,128)(2,1)}), bf16[2048,2048]{1,0:T(8,128)(2,1)}) %reduce-scatter.15.cloned.1.call-update) | async-done | bytes 8388624
  6711.1 975.3 %all-reduce.21 = (f32[512]{0:T(512)}, f32[512]{0:T(512)}, f32[512,6144]{1,0:T(8,128)}, f32[512]{0:T(512)}, f32[512]{0:T(512)}, /*index=5*/f32[512,2048]{1,0:T(8,...) all-reduce(f32[512]{0:T(512)S(1)} %dynamic-slice_convert_fusion.8, ...), channel_id=1, replica_groups=mesh['fsdp'=4,'replica'=2,'ctx'=4] {'replica','ctx'}, use_global_device_ids=true, to_apply=%region_26.27 | all-reduce | flops 12589056 | bytes 75546624 | tf_op jit(solution)/shard_map/psum | solution.py:339
  (352 shorter events, 296.7 us)
Async XLA Ops:
  7.2 95.6 %copy-start.3 = (bf16[1,272,2048]{2,1,0:T(8,128)(2,1)S(1)}, bf16[1,272,2048]{2,1,0:T(8,128)(2,1)}, u32[]{:S(2)}) copy-start(bf16[1,272,2048]{2,1,0:T(8,128)(2,1)} %param.21) | copy-start | bytes 3342340
  7.2 430.2 %all-gather.17.cloned.1.call-start = ((), (), s32[]{:S(2)}) async-start(), calls=%async_computation.4 | async-start | bytes 31457280 | tf_op jit(solution)/shard_map/all_gather | solution.py:92
  7.9 503.1 %all-gather.25.cloned.1.call-start = ((), (), s32[]{:S(2)}) async-start(), calls=%async_computation.10 | async-start | bytes 5570560 | tf_op jit(solution)/shard_map/all_gather | solution.py:144
  19.0 482.4 %copy-start.24 = (f32[4,1,512]{2,1,0:T(1,128)}, f32[4,1,512]{2,1,0:T(1,128)S(1)}, u32[]{:S(2)}) copy-start(f32[4,1,512]{2,1,0:T(1,128)S(1)} %convert_element_type.263) | copy-start | bytes 24580
  101.0 348.3 %copy-start.28 = (f32[272]{0:T(512)}, f32[272]{0:T(512)S(1)}, u32[]{:S(2)}) copy-start(f32[272]{0:T(512)S(1)} %broadcast_multiply_fusion.5) | copy-start | bytes 3268
  102.8 346.5 %copy-start.32 = (f32[272]{0:T(512)}, f32[272]{0:T(512)S(1)}, u32[]{:S(2)}) copy-start(f32[272]{0:T(512)S(1)} %add_rsqrt_fusion.1) | copy-start | bytes 3268
  103.3 346.0 %copy-start.18 = (bf16[272,2048]{1,0:T(8,128)(2,1)}, bf16[272,2048]{1,0:T(8,128)(2,1)S(1)}, u32[]{:S(2)}) copy-start(bf16[272,2048]{1,0:T(8,128)(2,1)S(1)} %fusion.45) | copy-start | bytes 3342340
  454.1 72.7 all-gather.27.cloned.1.call-start
  457.0 220.7 %all-gather.19.cloned.1.call-start = ((), (), s32[]{:S(2)}) async-start(), calls=%async_computation.5 | async-start | bytes 10485760 | tf_op jit(solution)/shard_map/all_gather | solution.py:95
  457.6 11.7 copy-start.48
  457.6 21.4 copy-start.49
  457.6 31.1 copy-start.42
  457.6 41.4 copy-start.52
  457.6 42.6 copy-start.17
  457.6 781.1 %all-gather.21.cloned.1.call-start = ((), (), s32[]{:S(2)}) async-start(), calls=%async_computation.6 | async-start | bytes 41943040 | tf_op jit(solution)/shard_map/all_gather | solution.py:99
  458.2 1341.6 %all-gather.23.cloned.1.call-start = ((), (), s32[]{:S(2)}) async-start(), calls=%async_computation.7 | async-start | bytes 41943040 | tf_op jit(solution)/shard_map/all_gather | solution.py:192
  458.8 5283.1 %reduce-scatter.11.cloned.1.call-start = ((), (), s32[]{:S(2)}) async-start(), calls=%async_computation.9 | async-start | bytes 10485760 | tf_op jit(solution)/shard_map/reduce_scatter | solution.py:320
  479.0 1373.6 %copy-start.26 = (f32[4,1,512]{2,1,0:T(1,128)}, f32[4,1,512]{2,1,0:T(1,128)S(1)}, u32[]{:S(2)}) copy-start(f32[4,1,512]{2,1,0:T(1,128)S(1)} %convert_element_type.268) | copy-start | bytes 24580
  488.7 750.1 %copy-start.38 = (f32[4,1,512]{2,1,0:T(1,128)}, f32[4,1,512]{2,1,0:T(1,128)S(1)}, u32[]{:S(2)}) copy-start(f32[4,1,512]{2,1,0:T(1,128)S(1)} %convert_element_type.269) | copy-start | bytes 24580
  589.0 95.3 %copy-start.1 = (pred[1,1,272,1138]{3,2,1,0:T(8,128)(4,1)}, pred[1,1,272,1138]{3,2,1,0:T(8,128)(4,1)S(1)}, u32[]{:S(2)}) copy-start(pred[1,1,272,1138]{3,2,1,0:T(8,128)(4,1)S(1)} %get-tuple-element.553) | copy-start | bytes 928612
  589.0 95.3 %copy-start.8 = (bf16[1,272,2048]{1,2,0:T(8,128)(2,1)}, bf16[1,272,2048]{1,2,0:T(8,128)(2,1)S(1)}, u32[]{:S(2)}) copy-start(bf16[1,272,2048]{1,2,0:T(8,128)(2,1)S(1)} %get-tuple-element.566) | copy-start | bytes 3342340
  684.3 1168.3 %copy-start.30 = (f32[272]{0:T(512)}, f32[272]{0:T(512)S(1)}, u32[]{:S(2)}) copy-start(f32[272]{0:T(512)S(1)} %broadcast_multiply_fusion.4) | copy-start | bytes 3268
  686.1 1166.6 %copy-start.36 = (f32[272]{0:T(512)}, f32[272]{0:T(512)S(1)}, u32[]{:S(2)}) copy-start(f32[272]{0:T(512)S(1)} %add_rsqrt_fusion) | copy-start | bytes 3268
  1238.8 561.0 %copy-start.13 = (bf16[1,272,2048]{2,1,0:T(8,128)(2,1)S(1)}, bf16[1,272,2048]{2,1,0:T(8,128)(2,1)}, u32[]{:S(2)}) copy-start(bf16[1,272,2048]{2,1,0:T(8,128)(2,1)} %param.24) | copy-start | bytes 3342340
  1799.8 35.5 copy-start.6
  1835.3 17.3 copy-start.53
  1835.3 17.3 copy-start.14
  1863.1 3878.7 %reduce-scatter.9.cloned.1.call-start = ((), (), s32[]{:S(2)}) async-start(), calls=%async_computation.8 | async-start | bytes 31457280 | tf_op jit(solution)/shard_map/reduce_scatter | solution.py:311
  2055.8 11.4 slice-start.2
  2055.9 11.4 slice-start.3
  2055.9 11.4 slice-start.4
  4609.9 11.2 copy-start.11
  4610.0 13.1 copy-start.20
  4610.1 12.9 copy-start.21
  4645.3 1510.8 %reduce-scatter.13.cloned.1.call-start = ((), (), s32[]{:S(2)}) async-start(), calls=%async_computation.12 | async-start | bytes 41943040
  4671.3 2039.8 %reduce-scatter.15.cloned.1.call-start = ((), (), s32[]{:S(2)}) async-start(), calls=%async_computation.13 | async-start | bytes 41943040
  4696.4 408.3 %copy-start.51 = (u32[32]{0:T(128)S(1)}, u32[32]{0:T(128)}, u32[]{:S(2)}) copy-start(u32[32]{0:T(128)} %constant.195) | copy-start | bytes 388
  4696.4 410.2 %copy-start.50 = (bf16[512]{0:T(512)(128)(2,1)S(1)}, bf16[512]{0:T(512)(128)(2,1)}, u32[]{:S(2)}) copy-start(bf16[512]{0:T(512)(128)(2,1)} %param.37) | copy-start | bytes 3076
  4696.4 363.9 %collective-permute-start = (bf16[2048,2048]{1,0:T(8,128)(2,1)}, bf16[2048,2048]{1,0:T(8,128)(2,1)}, u32[]{:S(2)}, u32[]{:S(2)}) collective-permute-start(bf16[2048,2048]{1,0:T(8,128)(2,1)} %param.36), channel_id=1, source_target_pairs={{0,8},{8,16},{16,24},{24,0},{1,9},{9,17},{17,25},{25,1},{2,10},{10... | collective-permute-start | bytes 25165832 | tf_op jit(solution)/shard_map/ppermute | solution.py:22
  5060.3 541.2 %collective-permute-start.1 = (bf16[2048,2048]{1,0:T(8,128)(2,1)}, bf16[2048,2048]{1,0:T(8,128)(2,1)}, u32[]{:S(2)}, u32[]{:S(2)}) collective-permute-start(bf16[2048,2048]{1,0:T(8,128)(2,1)} %collective-permute-done), channel_id=1, source_target_pairs={{0,8},{8,16},{16,24},{24,0},{1,9},{9,17},{17,25},{25,1},{2,10},{10... | collective-permute-start | bytes 25165832 | tf_op jit(solution)/shard_map/ppermute | solution.py:22
  5103.1 523.6 %collective-permute-start.2 = (bf16[2048,2048]{1,0:T(8,128)(2,1)}, bf16[2048,2048]{1,0:T(8,128)(2,1)}, u32[]{:S(2)}, u32[]{:S(2)}) collective-permute-start(bf16[2048,2048]{1,0:T(8,128)(2,1)} %param.36), channel_id=1, source_target_pairs={{0,24},{8,0},{16,8},{24,16},{1,25},{9,1},{17,9},{25,17},{2,26},{10... | collective-permute-start | bytes 25165832 | tf_op jit(solution)/shard_map/ppermute | solution.py:24
  5668.4 19.2 copy-start.4
  5668.4 19.2 copy-start.29
  5668.4 19.2 copy-start.33
  5687.6 14.9 copy-start.34
  5687.6 14.9 copy-start.35
  5687.6 14.9 copy-start.43
  5687.6 14.9 copy-start.44
  (33 other events, 155.7 us)
Sparse Core Ops, SparseCore 0:
  9.6 427.7 all-gather.16
  454.2 34.3 all-gather.24
  490.8 35.9 all-gather.26
  528.2 149.4 all-gather.18
  679.1 559.6 all-gather.20
  1240.2 559.5 all-gather.22
  1863.2 142.2 reduce-scatter.10
  4645.4 844.9 reduce-scatter.8
  5492.9 663.0 reduce-scatter.12
  6158.2 552.7 reduce-scatter.14
